TPU v7x, 32 devices: a whole 2x2x4 slice. The times are simulated.
32 devices in a mesh: band: 4 (over y, x), dom: 8 (over z, core).
Axes of the slice: x: 2, y: 2, z: 4, core: 2. Of those that a mesh axis runs over, the one named last changes fastest.
Arguments:
- orbitals: float32 [1024, 32768], P('band', 'dom'), may hold values from -6 to 6
- projectors: float32 [256, 512, 128], P('dom'), may hold values from -0.25 to 0.25
- window_start: int32 [256], P('dom'), may hold values from 0 to 3584
- slot_atom: int32 [8, 32], replicated, may hold values from 0 to 23, as said below
- atom_home: int32 [24], replicated, may hold values from 0 to 23, as said below
- atom_matrices: float32 [24, 128, 128], P('dom'), may hold values from -0.1875 to 0.1875
- rotation: float32 [1024, 1024], P('band'), may hold values from -0.1875 to 0.1875
Outputs:
- rotated: float32 [1024, 32768], P('band', 'dom')
Inputs may be any that keep to these rules, and one draw needn't show every extreme that they name: `atom_home`: a permutation; atom a is owned by domain atom_home[a] // 3, so every domain owns 3 atoms. `slot_atom`: in one domain at most 8 windows have atoms of one owner; in every domain some owner has exactly 8 of them, and some owner has exactly 8 from every domain.
All inputs are finite; a program needn't handle non-finite values.
Results may differ from a plain program's by a relative error of at most 0.0003.
Values sent between devices are 32-bit elements; how exact they have to be, the bound alone decides.
No kernel may reach another device: no remote copies, remote signals or barrier semaphores. Data moves between devices by JAX's collectives and lax.ppermute only.
A program may use at most 128 MiB of HBM per device.

v0:
```python
import jax
import jax.numpy as jnp
from jax import lax
from jax.sharding import PartitionSpec as P

HIGHEST = lax.Precision.HIGHEST


def per_device(orbitals, projectors, window_start, slot_atom, atom_home, atom_matrices, rotation):
    own_domain = lax.axis_index("dom")
    slot_count = projectors.shape[0]
    window = projectors.shape[1]
    atom_count = atom_home.shape[0]
    columns = rotation
    base_field = jnp.dot(
        columns,
        lax.all_gather(orbitals, "band", axis=0, tiled=True),
        precision=HIGHEST,
        preferred_element_type=jnp.float32,
    )
    windows = jax.vmap(lambda offset: lax.dynamic_slice_in_dim(orbitals, offset, window, 1))(
        window_start
    )
    partials = jnp.einsum("sbw,swp->sbp", windows, projectors, precision=HIGHEST)
    atom_ids = jnp.arange(atom_count, dtype=jnp.int32)
    home_table = jnp.sum(
        jnp.where(slot_atom[:, :, None] == atom_ids[None, None, :], atom_home[None, None, :], 0),
        axis=2,
    )
    own_home = lax.dynamic_index_in_dim(home_table, own_domain, 0, keepdims=False)
    home_match = (atom_ids[:, None] == own_home[None, :]).astype(jnp.float32)
    per_atom = jnp.einsum("rs,sbp->rbp", home_match, partials, precision=HIGHEST)
    owned_sums = lax.psum_scatter(per_atom, "dom", scatter_dimension=0, tiled=True)
    owned_factors = jnp.einsum("abp,apq->abq", owned_sums, atom_matrices, precision=HIGHEST)
    columns = rotation
    owned_factors = jnp.einsum(
        "bc,scp->sbp",
        columns,
        lax.all_gather(owned_factors, "band", axis=1, tiled=True),
        precision=HIGHEST,
    )
    all_factors = lax.all_gather(owned_factors, "dom", axis=0, tiled=True)
    slot_factors = jnp.einsum("rs,rbp->sbp", home_match, all_factors, precision=HIGHEST)
    updates = jnp.einsum("sbq,swq->sbw", slot_factors, projectors, precision=HIGHEST)

    def add_window(slot_index, current):
        offset = window_start[slot_index]
        previous = lax.dynamic_slice_in_dim(current, offset, window, 1)
        return lax.dynamic_update_slice_in_dim(current, previous + updates[slot_index], offset, 1)

    corrected = lax.fori_loop(0, slot_count, add_window, base_field)
    return corrected


def solution(mesh):
    in_specs = (
        P("band", "dom"),
        P("dom", None, None),
        P("dom"),
        P(),
        P(),
        P("dom", None, None),
        P("band", None),
    )
    out_specs = P("band", "dom")
    return jax.shard_map(
        per_device, mesh=mesh, in_specs=in_specs, out_specs=out_specs, check_vma=False
    )
```

profile of v0, /device:TPU:0, one launch (start us, length us, event | category | flops | bytes accessed | tf_op | source)
XLA Modules:
  0.0 689.3 jit_solution(3986818245490201017)
XLA Ops:
  7.3 107.7 %while.15 = (s32[]{:T(128)}, f32[256,4096]{1,0:T(8,128)}, s32[32,2]{0,1:T(2,128)S(1)}, f32[32,256,512]{2,1,0:T(8,128)}, s32[]{:T(128)}) while((s32[]{:T(128)}, f32[256,4096]{1,0:T(8,128)}, s32[32,2]{0,1:T(2,128)S(1)}, f32[32,256,512]{2,1,0:T(8,128)}, s32[]{:T(128)}) %tuple.39), condition=%wide.while_cond, body=%wide.while_body.sunk | while | flops 2 | bytes 1049689 | solution.py:21
  115.1 19.3 %fusion.14 = f32[32,256,128]{2,1,0:T(8,128)S(1)} fusion(f32[32,256,512]{2,1,0:T(8,128)} %get-tuple-element.92, f32[32,512,128]{2,1,0:T(8,128)} %param.10), kind=kOutput, calls=%fused_computation.21 | convolution fusion | flops 6442450944 | bytes 29360128 | tf_op jit(solution)/shard_map/sbw,swp->sbp/dot_general | solution.py:24
  134.4 4.3 fusion.2
  141.0 43.3 %reduce-scatter.2.cloned.1.call-done = f32[3,256,128]{2,1,0:T(8,128)} async-done(((f32[24,256,128]{2,1,0:T(8,128)}), f32[3,256,128]{2,1,0:T(8,128)}) %reduce-scatter.2.cloned.1.call-update) | async-done | bytes 393232 | tf_op jit(solution)/shard_map/reduce_scatter | solution.py:33
  186.7 30.0 %all-gather.6.cloned.1.call-done = f32[3,1024,128]{2,1,0:T(8,128)} async-done(((f32[3,256,128]{2,1,0:T(8,128)}), f32[3,1024,128]{2,1,0:T(8,128)}) %all-gather.6.cloned.1.call-update) | async-done | bytes 1572880 | tf_op jit(solution)/shard_map/all_gather | solution.py:39
  216.7 4.0 convolution_bitcast_fusion
  222.3 37.8 %all-gather.8.cloned.1.call-done = f32[24,256,128]{2,1,0:T(8,128)} async-done(((f32[3,256,128]{2,1,0:T(8,128)}), f32[24,256,128]{2,1,0:T(8,128)}) %all-gather.8.cloned.1.call-update) | async-done | bytes 3145744 | tf_op jit(solution)/shard_map/all_gather | solution.py:42
  260.1 5.8 fusion.4
  265.9 21.7 %fusion = f32[32,256,512]{2,1,0:T(8,128)} fusion(f32[32,512,128]{2,1,0:T(8,128)} %param.10, f32[32,256,128]{2,0,1:T(8,128)S(1)} %fusion.4), kind=kOutput, calls=%fused_computation.3 | convolution fusion | flops 6442450944 | bytes 29360128 | tf_op jit(solution)/shard_map/sbq,swq->sbw/dot_general | solution.py:44
  287.6 130.4 %all-gather.4.cloned.1.call-done = f32[1024,4096]{1,0:T(8,128)} async-done(((f32[256,4096]{1,0:T(8,128)}), f32[1024,4096]{1,0:T(8,128)}) %all-gather.4.cloned.1.call-update) | async-done | bytes 16777232 | tf_op jit(solution)/shard_map/all_gather | solution.py:17
  418.0 18.0 %fusion.13 = f32[256,4096]{1,0:T(8,128)} fusion(f32[256,1024]{1,0:T(8,128)S(1)} %copy-done, f32[1024,4096]{1,0:T(8,128)} %all-gather.4.cloned.1.call-done), kind=kOutput, calls=%fused_computation.20 | convolution fusion | flops 12884901888 | bytes 22020096 | tf_op jit(solution)/shard_map/dot_general | solution.py:15
  436.0 246.8 %while.14 = (s32[]{:T(128)}, f32[256,4096]{1,0:T(8,128)}, s32[32]{0:T(128)S(1)}, f32[32,256,512]{2,1,0:T(8,128)}, s32[]{:T(128)}, /*index=5*/s32[]{:T(128)}, s32[]{:T(128)}) while((s32[]{:T(128)}, f32[256,4096]{1,0:T(8,128)}, s32[32]{0:T(128)S(1)}, f32[32,256,512]{2,1,0:T(8,128)}, s32[]{:T(128)}, /*index=5*/s32[]{:T(128)}, s32[]{:T(128)}) %tuple.53), condition=%wide.region_3.4_spmd, body=%wide.region_2.3_spmd.sunk | while | flops 131077 | bytes 2621575 | solution.py:51
  439.9 3.8 dynamic_update_slice.8
  447.6 3.8 dynamic_update_slice.8
  455.4 3.8 dynamic_update_slice.8
  463.1 3.8 dynamic_update_slice.8
  470.8 3.8 dynamic_update_slice.8
  478.5 3.8 dynamic_update_slice.8
  486.2 3.8 dynamic_update_slice.8
  509.2 3.8 dynamic_update_slice.8
  540.1 3.8 dynamic_update_slice.8
  547.8 3.8 dynamic_update_slice.8
  609.5 3.8 dynamic_update_slice.8
  617.2 3.8 dynamic_update_slice.8
  (206 shorter events, 256.6 us)
Async XLA Ops:
  6.5 210.2 %copy-start = (f32[256,1024]{1,0:T(8,128)S(1)}, f32[256,1024]{1,0:T(8,128)}, u32[]{:S(2)}) copy-start(f32[256,1024]{1,0:T(8,128)} %param.15) | copy-start | bytes 3145732
  6.5 108.5 %copy-start.2 = (s32[8,32]{1,0:T(8,128)S(1)}, s32[8,32]{1,0:T(8,128)}, u32[]{:S(2)}) copy-start(s32[8,32]{1,0:T(8,128)} %param.12) | copy-start | bytes 3076
  6.5 108.5 %copy-start.3 = (s32[24]{0:T(128)S(1)}, s32[24]{0:T(128)}, u32[]{:S(2)}) copy-start(s32[24]{0:T(128)} %param.13) | copy-start | bytes 292
  6.5 177.7 %reduce-scatter.2.cloned.1.call-start = ((), (), s32[]{:S(2)}) async-start(), calls=%async_computation.2 | async-start | bytes 3538944 | tf_op jit(solution)/shard_map/reduce_scatter | solution.py:33
  138.7 45.6 %copy-start.1 = (f32[3,128,128]{2,1,0:T(8,128)S(1)}, f32[3,128,128]{2,1,0:T(8,128)}, u32[]{:S(2)}) copy-start(f32[3,128,128]{2,1,0:T(8,128)} %param.14) | copy-start | bytes 589828
  140.9 75.8 %all-gather.6.cloned.1.call-start = ((), (), s32[]{:S(2)}) async-start(), calls=%async_computation.3 | async-start | bytes 1966080 | tf_op jit(solution)/shard_map/all_gather | solution.py:39
  186.5 73.6 %all-gather.8.cloned.1.call-start = ((), (), s32[]{:S(2)}) async-start(), calls=%async_computation.4 | async-start | bytes 3538944 | tf_op jit(solution)/shard_map/all_gather | solution.py:42
  221.7 196.3 %all-gather.4.cloned.1.call-start = ((), (), s32[]{:S(2)}) async-start(), calls=%async_computation.1 | async-start | bytes 20971520 | tf_op jit(solution)/shard_map/all_gather | solution.py:17
  287.6 148.4 %copy-start.4 = (s32[32]{0:T(128)S(1)}, s32[32]{0:T(128)}, u32[]{:S(2)}) copy-start(s32[32]{0:T(128)} %param.11) | copy-start | bytes 388
Sparse Core Ops, SparseCore 0:
  141.1 43.1 reduce-scatter.1
  186.6 30.0 all-gather.5
  221.8 38.2 all-gather.7
  261.8 156.1 all-gather.3
where the time goes:
time: 695 us; the launch traced here: 689 us
  local copies, waits for them, and re-layouts  251 us (36%)
  waiting for transfers between devices  242 us (35%)
  matrix products  75.2 us (11%)
  loops' own time  59.9 us (9%)
  other arithmetic  47.5 us (7%)
  between operations  13.2 us (2%)
    all_gather x1, waiting for transfers between devices, per_device(): lax.all_gather(orbitals, 'band', axis=0, tiled=True)  130 us
    dynamic_update_slice x32, local copies, waits for them, and re-layouts, add_window(): lax.dynamic_update_slice_in_dim(current, previous + updates[slot_index],...  120 us
    gather x96, local copies, waits for them, and re-layouts  108 us
    another operation x1, loops' own time, per_device(): corrected = lax.fori_loop(0, slot_count, add_window, base_field)  59.9 us
    add x32, other arithmetic, add_window(): previous + updates[slot_index]  46.6 us
    reduce_scatter x1, waiting for transfers between devices, per_device(): lax.psum_scatter(per_atom, 'dom', scatter_dimension=0, tiled=True)  43.3 us
    all_gather x1, waiting for transfers between devices, per_device(): all_factors = lax.all_gather(owned_factors, 'dom', axis=0, tiled=True)  37.8 us
    all_gather x1, waiting for transfers between devices, per_device(): lax.all_gather(owned_factors, 'band', axis=1, tiled=True)  30 us
  transfers between devices with their start and end apart: 4, of which 4 were waited for; matrix products, arithmetic and copies ran while one was open for 4% of the time, Pallas kernels for 0%

commit v1 on v0

--- a/solution.py
+++ b/solution.py
@@ -4,6 +4,23 @@
 from jax.sharding import PartitionSpec as P
 
 HIGHEST = lax.Precision.HIGHEST
+
+
+def points_derive(content, net_axis):
+    response = lax.axis_size(net_axis)
+    right_arr = lax.axis_index(net_axis)
+    tmp, wide_out = (response, right_arr)
+    z2, h_now = (content, 1)
+    while h_now < tmp:
+        entries = []
+        for m in range(tmp):
+            entries.append((m, m ^ h_now))
+        now = lax.ppermute(z2, net_axis, entries)
+        block_next = jnp.concatenate([z2, now], axis=0)
+        left_arr = jnp.concatenate([now, z2], 0)
+        z2 = jnp.where(wide_out & h_now == 0, block_next, left_arr)
+        h_now = 2 * h_now
+    return z2
 
 
 def per_device(orbitals, projectors, window_start, slot_atom, atom_home, atom_matrices, rotation):
@@ -14,7 +31,7 @@
     columns = rotation
     base_field = jnp.dot(
         columns,
-        lax.all_gather(orbitals, "band", axis=0, tiled=True),
+        points_derive(orbitals, "band"),
         precision=HIGHEST,
         preferred_element_type=jnp.float32,
     )

time: 695 us -> 764 us (1.099)
  waiting for transfers between devices: 242 us -> 276 us
  matrix products: 75.2 us -> 89.4 us
  other arithmetic: 47.5 us -> 57.8 us
    ppermute x0 -> x2, waiting for transfers between devices: none -> 232 us  [points_derive(): now = lax.ppermute(z2, net_axis, entries)]
    all_gather x1 -> x0, waiting for transfers between devices: 130 us -> none  [per_device(): lax.all_gather(orbitals, 'band', axis=0, tiled=True)]
    reduce_scatter x1, waiting for transfers between devices: 43.3 us -> 0.01 us  [per_device(): lax.psum_scatter(per_atom, 'dom', scatter_dimension=0, tiled=True)]
    all_gather x1, waiting for transfers between devices: 37.8 us -> 0.01 us  [per_device(): all_factors = lax.all_gather(owned_factors, 'dom', axis=0, tiled=True)]
    dot_general x1, matrix products: 18 us -> 32.9 us  [per_device(): jnp.dot(columns, points_derive(orbitals, 'band'), precision=HIGHEST, pref...]
    all_gather x1, waiting for transfers between devices: 30 us -> 44.1 us  [per_device(): lax.all_gather(owned_factors, 'band', axis=1, tiled=True)]
    select_n x0 -> x1, other arithmetic: none -> 9.62 us  [points_derive(): z2 = jnp.where(wide_out & h_now == 0, block_next, left_arr)]
  transfers between devices with their start and end apart: 4 -> 5, of which waited for: 4 -> 3; matrix products, arithmetic and copies ran while one was open for 4% -> 7% of each run, Pallas kernels for 0% -> 0%
where the time goes in v1:
time: 764 us; the launch traced here: 758 us
  waiting for transfers between devices  276 us (36%)
  local copies, waits for them, and re-layouts  255 us (33%)
  matrix products  89.4 us (12%)
  loops' own time  61.3 us (8%)
  other arithmetic  57.8 us (8%)
  between operations  13.2 us (2%)
    ppermute x2, waiting for transfers between devices, points_derive(): now = lax.ppermute(z2, net_axis, entries)  232 us
    dynamic_update_slice x32, local copies, waits for them, and re-layouts, add_window(): lax.dynamic_update_slice_in_dim(current, previous + updates[slot_index],...  120 us
    gather x96, local copies, waits for them, and re-layouts  107 us
    another operation x1, loops' own time, per_device(): corrected = lax.fori_loop(0, slot_count, add_window, base_field)  61.3 us
    add x32, other arithmetic, add_window(): previous + updates[slot_index]  46.6 us
    all_gather x1, waiting for transfers between devices, per_device(): lax.all_gather(owned_factors, 'band', axis=1, tiled=True)  44.1 us
    dot_general x1, matrix products, per_device(): jnp.dot(columns, points_derive(orbitals, 'band'), precision=HIGHEST, pref...  32.9 us
    dot_general x1, matrix products, per_device(): jnp.einsum('sbq,swq->sbw', slot_factors, projectors, precision=HIGHEST)  20.9 us
  transfers between devices with their start and end apart: 5, of which 3 were waited for; matrix products, arithmetic and copies ran while one was open for 7% of the time, Pallas kernels for 0%

profile of v1, /device:TPU:0, one launch (start us, length us, event | category | flops | bytes accessed | tf_op | source)
XLA Modules:
  0.0 758.2 jit_solution(10468257612858746101)
XLA Ops:
  7.3 107.1 %while.15 = (s32[]{:T(128)}, f32[256,4096]{1,0:T(8,128)}, s32[32,2]{0,1:T(2,128)S(1)}, f32[32,256,512]{2,1,0:T(8,128)}, s32[]{:T(128)}) while((s32[]{:T(128)}, f32[256,4096]{1,0:T(8,128)}, s32[32,2]{0,1:T(2,128)S(1)}, f32[32,256,512]{2,1,0:T(8,128)}, s32[]{:T(128)}) %tuple.43), condition=%wide.while_cond, body=%wide.while_body.sunk | while | flops 2 | bytes 1049689 | solution.py:38
  115.2 19.3 %fusion.22 = f32[32,256,128]{2,1,0:T(8,128)S(1)} fusion(f32[32,256,512]{2,1,0:T(8,128)} %get-tuple-element.92, f32[32,512,128]{2,1,0:T(8,128)} %param.10), kind=kOutput, calls=%fused_computation.31 | convolution fusion | flops 6442450944 | bytes 29360128 | tf_op jit(solution)/shard_map/sbw,swp->sbp/dot_general | solution.py:41
  134.5 4.3 fusion.10
  144.3 90.8 %collective-permute-done = f32[256,4096]{1,0:T(8,128)} collective-permute-done((f32[256,4096]{1,0:T(8,128)}, f32[256,4096]{1,0:T(8,128)}, u32[]{:S(2)}, u32[]{:S(2)}) %collective-permute-start) | collective-permute-done | bytes 4194336 | tf_op jit(solution)/shard_map/ppermute | solution.py:18
  235.1 9.6 %maximum_select_fusion.2 = f32[512,4096]{1,0:T(8,128)} fusion(f32[256,4096]{1,0:T(8,128)} %collective-permute-done, f32[256,4096]{1,0:T(8,128)} %get-tuple-element.216, pred[]{:T(512)S(6)} %eq.35), kind=kLoop, calls=%fused_computation.10 | loop fusion | flops 6291456 | bytes 16777216 | tf_op jit(solution)/shard_map/jit(_where)/select_n | solution.py:21
  248.8 44.1 %all-gather.3.cloned.1.call-done = f32[3,1024,128]{2,1,0:T(8,128)} async-done(((f32[3,256,128]{2,1,0:T(8,128)}), f32[3,1024,128]{2,1,0:T(8,128)}) %all-gather.3.cloned.1.call-update) | async-done | bytes 1572880 | tf_op jit(solution)/shard_map/all_gather | solution.py:56
  292.9 4.0 convolution_bitcast_fusion
  297.9 141.4 %collective-permute-done.1 = f32[512,4096]{1,0:T(8,128)} collective-permute-done((f32[512,4096]{1,0:T(8,128)}, f32[512,4096]{1,0:T(8,128)}, u32[]{:S(2)}, u32[]{:S(2)}) %collective-permute-start.1) | collective-permute-done | bytes 8388640 | tf_op jit(solution)/shard_map/ppermute | solution.py:18
  439.3 32.9 %fusion.7 = f32[256,4096]{0,1:T(8,128)} fusion(f32[256,1024]{1,0:T(8,128)S(1)} %copy-done, f32[512,4096]{1,0:T(8,128)} %collective-permute-done.1, f32[512,4096]{1,0:T(8,128)} %maximum_select_fusion.2, pred[]{:T(512)S(6)} %eq.34), kind=kOutput, calls=%fused_computation.12 | convolution fusion | flops 12897484800 | bytes 22020096 | tf_op jit(solution)/shard_map/dot_general | solution.py:32
  472.1 5.6 copy.23
  477.7 5.8 fusion.12
  483.6 20.9 %fusion.8 = f32[32,256,512]{2,1,0:T(8,128)} fusion(f32[32,512,128]{2,1,0:T(8,128)} %param.10, f32[32,256,128]{2,0,1:T(8,128)S(1)} %fusion.12), kind=kOutput, calls=%fused_computation.13 | convolution fusion | flops 6442450944 | bytes 29360128 | tf_op jit(solution)/shard_map/sbq,swq->sbw/dot_general | solution.py:61
  504.5 247.1 %while.14 = (s32[]{:T(128)}, f32[256,4096]{1,0:T(8,128)}, s32[32]{0:T(128)S(1)}, f32[32,256,512]{2,1,0:T(8,128)}, s32[]{:T(128)}, /*index=5*/s32[]{:T(128)}, s32[]{:T(128)}) while((s32[]{:T(128)}, f32[256,4096]{1,0:T(8,128)}, s32[32]{0:T(128)S(1)}, f32[32,256,512]{2,1,0:T(8,128)}, s32[]{:T(128)}, /*index=5*/s32[]{:T(128)}, s32[]{:T(128)}) %tuple.55), condition=%wide.region_3.4_spmd, body=%wide.region_2.3_spmd.sunk | while | flops 131077 | bytes 2621575 | solution.py:68
  508.5 3.8 dynamic_update_slice.8
  516.2 3.8 dynamic_update_slice.8
  523.9 3.8 dynamic_update_slice.8
  531.7 3.8 dynamic_update_slice.8
  539.4 3.8 dynamic_update_slice.8
  547.1 3.8 dynamic_update_slice.8
  593.3 3.8 dynamic_update_slice.8
  616.5 3.8 dynamic_update_slice.8
  678.3 3.8 dynamic_update_slice.8
  701.5 3.8 dynamic_update_slice.8
  740.2 3.8 dynamic_update_slice.8
  (207 shorter events, 263.7 us)
Async XLA Ops:
  6.5 286.4 %copy-start = (f32[256,1024]{1,0:T(8,128)S(1)}, f32[256,1024]{1,0:T(8,128)}, u32[]{:S(2)}) copy-start(f32[256,1024]{1,0:T(8,128)} %param.15) | copy-start | bytes 3145732
  6.5 240.0 %reduce-scatter.2.cloned.1.call-start = ((), (), s32[]{:S(2)}) async-start(), calls=%async_computation.1 | async-start | bytes 3538944 | tf_op jit(solution)/shard_map/reduce_scatter | solution.py:50
  141.0 151.9 %all-gather.3.cloned.1.call-start = ((), (), s32[]{:S(2)}) async-start(), calls=%async_computation.2 | async-start | bytes 1966080 | tf_op jit(solution)/shard_map/all_gather | solution.py:56
  141.2 93.9 %collective-permute-start = (f32[256,4096]{1,0:T(8,128)}, f32[256,4096]{1,0:T(8,128)}, u32[]{:S(2)}, u32[]{:S(2)}) collective-permute-start(f32[256,4096]{1,0:T(8,128)} %get-tuple-element.216), channel_id=1, source_target_pairs={{0,8},{8,0},{16,24},{24,16},{1,9},{9,1},{17,25},{25,17},{2,10},{10... | collective-permute-start | bytes 12582920 | tf_op jit(solution)/shard_map/ppermute | solution.py:18
  144.3 102.2 %copy-start.2 = (f32[3,128,128]{2,1,0:T(8,128)S(1)}, f32[3,128,128]{2,1,0:T(8,128)}, u32[]{:S(2)}) copy-start(f32[3,128,128]{2,1,0:T(8,128)} %param.14) | copy-start | bytes 589828
  244.7 194.5 %collective-permute-start.1 = (f32[512,4096]{1,0:T(8,128)}, f32[512,4096]{1,0:T(8,128)}, u32[]{:S(2)}, u32[]{:S(2)}) collective-permute-start(f32[512,4096]{1,0:T(8,128)} %maximum_select_fusion.2), channel_id=1, source_target_pairs={{0,16},{8,24},{16,0},{24,8},{1,17},{9,25},{17,1},{25,9},{2,18},{10... | collective-permute-start | bytes 25165832 | tf_op jit(solution)/shard_map/ppermute | solution.py:18
  248.8 229.0 %all-gather.5.cloned.1.call-start = ((), (), s32[]{:S(2)}) async-start(), calls=%async_computation.3 | async-start | bytes 3538944 | tf_op jit(solution)/shard_map/all_gather | solution.py:59
  483.6 20.9 %copy-start.3 = (s32[32]{0:T(128)S(1)}, s32[32]{0:T(128)}, u32[]{:S(2)}) copy-start(s32[32]{0:T(128)} %param.11) | copy-start | bytes 388
  483.6 268.0 %copy-start.1 = (f32[256,1024]{1,0:T(8,128)S(1)}, f32[256,1024]{1,0:T(8,128)}, u32[]{:S(2)}) copy-start(f32[256,1024]{1,0:T(8,128)} %param.15) | copy-start | bytes 3145732
Sparse Core Ops, SparseCore 0:
  141.1 43.0 reduce-scatter.1
  248.9 43.9 all-gather.2
  298.0 38.2 all-gather.4
